TPU v7x, 512 devices: a whole 4x8x8 slice. The times are simulated.
512 devices in a mesh: blk: 8 (over y_lo, core), leaf: 64 (over z, y_hi, x).
Axes of the slice: x: 4, y: 8 (y_hi: 2, y_lo: 4; y = y_hi * 4 + y_lo), z: 8, core: 2. Of those that a mesh axis runs over, the one named last changes fastest.
Arguments:
- positions: float32 [3, 64, 8, 128], P(None, 'leaf', 'blk'), may hold values from 0 to 32, as said below
- panel_areas: float32 [64, 8, 128], P('leaf', 'blk'), may hold values from 0.5 to 2
- probe_cols: bfloat16 [576, 64, 8, 128], P(None, 'leaf', 'blk'), may hold values from -5 to 5
- full_sketch: bfloat16 [576, 64, 8, 128], P(None, 'leaf', 'blk'), may hold values from -3 to 3
- tree_order: int32 [64, 8, 128], P('leaf', 'blk'), may hold values from 0 to 127, each once within a row
- leaf_basis: bfloat16 [64, 8, 128, 512], P('leaf', 'blk'), may hold values from -0.1875 to 0.1875
- transfer_mats: bfloat16 [64, 3, 512, 512], P('leaf'), may hold values from -0.1875 to 0.1875
Outputs:
- offdiag_sketch: bfloat16 [576, 64, 8, 128], P(None, 'leaf', 'blk')
- nested_sketch: float32 [64, 2, 576, 512], P('leaf')
Inputs may be any that keep to these rules, and one draw needn't show every extreme that they name: `positions`: each leaf's panel centres lie on a surface patch of 32 by 32 mean panel widths. `tree_order`: along the last dimension, each row names every one of the 128 panels of its block once.
All inputs are finite; a program needn't handle non-finite values.
Results may differ from a plain program's by a relative error of at most 0.0046.
Values sent between devices are 32-bit elements; how exact they have to be, the bound alone decides.
No kernel may reach another device: no remote copies, remote signals or barrier semaphores. Data moves between devices by JAX's collectives and lax.ppermute only.
A program may use at most 64 MiB of HBM per device.

v0:
```python
import math
import jax
import jax.numpy as jnp
from jax import lax
from jax.sharding import PartitionSpec as P

inv_four_pi = 1.0 / (4.0 * math.pi)


def partner(value, axis, bit):
    mask = 2**bit
    pairs = [(source, source ^ mask) for source in range(lax.axis_size(axis))]
    return lax.ppermute(value, axis, pairs)


def kernel_tile(target_pos, target_area, source_pos, source_area):
    distance = jnp.zeros((target_pos.shape[1], source_pos.shape[1]), jnp.float32)
    for component in range(3):
        gap = target_pos[component][:, None] - source_pos[component][None, :]
        distance = distance + gap * gap
    soft = distance + 0.5 * (target_area[:, None] + source_area[None, :])
    return (inv_four_pi * lax.rsqrt(soft)).astype(jnp.bfloat16)


def target_blocks(target_pos, target_area):
    panels = target_pos.shape[1]
    block_size = min(512, panels)
    block_count = panels // block_size
    pos_blocks = jnp.transpose(target_pos.reshape(3, block_count, block_size), (1, 0, 2))
    return (pos_blocks, target_area.reshape(block_count, block_size))


def near_block(target_pos, target_area, source_pos, source_area, source_scaled):
    pos_blocks, area_blocks = target_blocks(target_pos, target_area)

    def one_block(entry):
        block_pos, block_area = entry
        kernel = kernel_tile(block_pos, block_area, source_pos, source_area)
        return lax.dot_general(
            source_scaled, kernel, (((1,), (1,)), ((), ())), preferred_element_type=jnp.float32
        )

    sums = lax.map(one_block, (pos_blocks, area_blocks))
    return jnp.transpose(sums, (1, 0, 2)).reshape(source_scaled.shape[0], target_pos.shape[1])


def project(current, level_mat):
    return jnp.dot(current, level_mat.astype(jnp.float32), precision=lax.Precision.HIGHEST)


def climb_rows(rows, level_mats):
    for tree_level in range(level_mats.shape[0]):
        projected = project(rows, level_mats[tree_level])
        rows = projected + partner(projected, "leaf", tree_level)
    return rows


def shards(positions, panel_areas, probe_cols, full_sketch, tree_order, leaf_basis, transfer_mats):
    panels = positions.shape[3]
    probe_count = probe_cols.shape[0]
    basis_width = leaf_basis.shape[3]
    level_count = transfer_mats.shape[1]
    coords = positions.reshape(3, panels)
    area_row = panel_areas.reshape(1, panels)
    probe_flat = probe_cols.reshape(probe_count, panels)
    scaled = (area_row * probe_flat.astype(jnp.float32)).astype(jnp.bfloat16)
    sorting = tree_order.reshape(panels)
    basis_flat = leaf_basis.reshape(panels, basis_width)
    level_mats = transfer_mats.reshape(level_count, basis_width, basis_width)
    probe_part = jnp.dot(
        jnp.take(probe_flat, sorting, axis=1), basis_flat, preferred_element_type=jnp.float32
    )
    outgoing = jnp.concatenate([coords, area_row, scaled.astype(jnp.float32)], axis=0)
    piece = lax.all_gather(outgoing, "ylo", axis=1, tiled=True)
    piece = lax.all_gather(piece, "core", axis=1, tiled=True)
    near_sum = near_block(coords, area_row[0], piece[:3], piece[3], piece[4:].astype(jnp.bfloat16))
    offdiag = (full_sketch.reshape(probe_count, panels).astype(jnp.float32) - near_sum).astype(
        jnp.bfloat16
    )
    sketch_part = jnp.dot(
        jnp.take(offdiag, sorting, axis=1), basis_flat, preferred_element_type=jnp.float32
    )
    stacked = jnp.concatenate([sketch_part, probe_part], axis=0)
    mine = lax.psum_scatter(stacked, "core", scatter_dimension=0, tiled=True)
    mine = lax.psum_scatter(mine, "ylo", scatter_dimension=0, tiled=True)
    top = climb_rows(mine, level_mats)
    top = lax.all_gather(top, "ylo", axis=0, tiled=True)
    nested = lax.all_gather(top, "core", axis=0, tiled=True).reshape(2, probe_count, basis_width)[
        None
    ]
    return (offdiag.reshape(probe_count, 1, 1, panels), nested)


def solution(mesh):
    blk = mesh.shape["blk"]
    devices = mesh.devices.reshape(blk // 2, 2, mesh.shape["leaf"])
    split_mesh = jax.sharding.Mesh(devices, ("ylo", "core", "leaf"))
    blk_axes = ("ylo", "core")
    in_specs = (
        P(None, "leaf", blk_axes, None),
        P("leaf", blk_axes, None),
        P(None, "leaf", blk_axes, None),
        P(None, "leaf", blk_axes, None),
        P("leaf", blk_axes, None),
        P("leaf", blk_axes, None, None),
        P("leaf", None, None, None),
    )
    out_specs = (P(None, "leaf", blk_axes, None), P("leaf", None, None, None))
    return jax.shard_map(
        shards, mesh=split_mesh, in_specs=in_specs, out_specs=out_specs, check_vma=False
    )
```

profile of v0, /device:TPU:1, one launch (start us, length us, event | category | flops | bytes accessed | tf_op | source)
XLA Modules:
  0.0 263.4 jit_solution(10981654303635103576)
XLA Ops:
  7.2 0.0 copy-start
  7.2 0.0 all-gather.5.cloned.1.call-start
  7.2 0.8 copy.15
  8.0 0.8 copy.13
  8.8 0.0 copy-start.5
  8.8 1.1 copy.14
  9.9 0.7 fusion.25
  10.6 0.9 pad_maximum_fusion.1
  11.5 0.0 copy-start.3
  11.5 0.0 all-gather.5.cloned.1.call-update
  11.6 0.0 all-gather.7.cloned.1.call-start
  11.6 45.6 %all-gather.5.cloned.1.call-done = f32[580,512]{0,1:T(8,128)} async-done(((f32[580,128]{0,1:T(8,128)}), f32[580,512]{0,1:T(8,128)}) %all-gather.5.cloned.1.call-update) | async-done | bytes 1187856 | tf_op jit(solution)/shard_map/all_gather | solution.py:74
  57.2 0.0 all-gather.7.cloned.1.call-update
  57.2 0.0 reduce-scatter.3.cloned.1.call-start
  57.3 0.0 copy-done.5
  57.3 0.9 gather_fusion.1
  58.2 0.0 copy-done.3
  58.2 0.0 copy-done
  58.2 0.0 copy-start.2
  58.2 0.0 copy-start.4
  58.3 0.4 fusion.26
  58.7 21.1 %all-gather.7.cloned.1.call-done = f32[580,1024]{0,1:T(8,128)} async-done(((f32[580,512]{0,1:T(8,128)}), f32[580,1024]{0,1:T(8,128)}) %all-gather.7.cloned.1.call-update) | async-done | bytes 2375696 | tf_op jit(solution)/shard_map/all_gather | solution.py:75
  79.7 3.2 %slice_reduce_fusion.3 = (f32[1024]{0:T(1024)S(1)}, f32[1024]{0:T(1024)S(1)}, f32[1024]{0:T(1024)S(1)}, f32[1024]{0:T(1024)S(1)}) fusion(f32[580,1024]{0,1:T(8,128)} %all-gather.7.cloned.1.call-done), kind=kLoop, calls=%fused_computation.8 | loop fusion | bytes 32768 | tf_op jit(solution)/shard_map/while/body/eval_jaxpr/slice | solution.py:19
  82.9 0.0 copy-done.2
  82.9 0.0 copy-done.4
  82.9 3.6 %fusion.10 = (bf16[576,1,1,128]{3,0,2,1:T(8,128)(2,1)}, f32[576,128]{1,0:T(8,128)S(1)}) fusion(bf16[576,1,1,128]{3,0,2,1:T(8,128)(2,1)S(1)} %copy-done.2, f32[1024]{0:T(1024)S(1)} %get-tuple-element.18, f32[128]{0:T(128)S(1)} %bitcast.50, f32[1024]{0:T(1024)S(1)} %get-tuple-element.19, f32[128]{0:T(128)S(1)} %get-tuple-element.29, ...), kind=kOutput, calls=%fused_computation.23 | convolution fusion | flops 152920064 | bytes 1918976 | tf_op jit(solution)/shard_map/while/body/eval_jaxpr/dot_general | solution.py:39
  86.5 0.2 copy.16
  86.7 0.9 gather_fusion
  87.6 0.4 fusion.28
  88.0 1.6 pad_maximum_fusion
  89.6 0.0 copy-start.1
  89.6 0.0 reduce-scatter.3.cloned.1.call-update
  89.6 0.0 reduce-scatter.5.cloned.1.call-start
  89.7 19.3 %reduce-scatter.3.cloned.1.call-done = f32[576,512]{1,0:T(8,128)} async-done(((f32[1152,512]{1,0:T(8,128)}), f32[576,512]{1,0:T(8,128)}) %reduce-scatter.3.cloned.1.call-update) | async-done | bytes 1179664 | tf_op jit(solution)/shard_map/reduce_scatter | solution.py:84
  108.9 0.0 reduce-scatter.5.cloned.1.call-update
  109.0 0.0 all-gather.9.cloned.1.call-start
  109.0 39.9 %reduce-scatter.5.cloned.1.call-done = f32[144,512]{1,0:T(8,128)} async-done(((f32[576,512]{1,0:T(8,128)}), f32[144,512]{1,0:T(8,128)}) %reduce-scatter.5.cloned.1.call-update) | async-done | bytes 294928 | tf_op jit(solution)/shard_map/reduce_scatter | solution.py:85
  148.9 0.0 copy-done.1
  148.9 1.4 fusion.5
  150.2 3.1 %collective-permute-start = (f32[144,512]{1,0:T(8,128)S(1)}, f32[144,512]{1,0:T(8,128)S(1)}, u32[]{:S(2)}, u32[]{:S(2)}) collective-permute-start(f32[144,512]{1,0:T(8,128)S(1)} %fusion.5), channel_id=1, source_target_pairs={{0,1},{1,0},{2,3},{3,2},{4,5},{5,4},{6,7},{7,6},{8,9},{9,8},{10,11... | collective-permute-start | bytes 884744 | tf_op jit(solution)/shard_map/ppermute | solution.py:13
  153.3 6.5 %collective-permute-done = f32[144,512]{1,0:T(8,128)S(1)} collective-permute-done((f32[144,512]{1,0:T(8,128)S(1)}, f32[144,512]{1,0:T(8,128)S(1)}, u32[]{:S(2)}, u32[]{:S(2)}) %collective-permute-start) | collective-permute-done | bytes 294944 | tf_op jit(solution)/shard_map/ppermute | solution.py:13
  159.8 0.4 fusion.3
  160.2 4.6 %collective-permute-start.1 = (f32[144,512]{1,0:T(8,128)S(1)}, f32[144,512]{1,0:T(8,128)S(1)}, u32[]{:S(2)}, u32[]{:S(2)}) collective-permute-start(f32[144,512]{1,0:T(8,128)S(1)} %fusion.3), channel_id=1, source_target_pairs={{0,2},{1,3},{2,0},{3,1},{4,6},{5,7},{6,4},{7,5},{8,10},{9,11},{10,... | collective-permute-start | bytes 884744 | tf_op jit(solution)/shard_map/ppermute | solution.py:13
  164.9 5.6 %collective-permute-done.1 = f32[144,512]{1,0:T(8,128)S(1)} collective-permute-done((f32[144,512]{1,0:T(8,128)S(1)}, f32[144,512]{1,0:T(8,128)S(1)}, u32[]{:S(2)}, u32[]{:S(2)}) %collective-permute-start.1) | collective-permute-done | bytes 294944 | tf_op jit(solution)/shard_map/ppermute | solution.py:13
  170.4 0.4 fusion.1
  170.8 6.3 %collective-permute-start.2 = (f32[144,512]{1,0:T(8,128)S(1)}, f32[144,512]{1,0:T(8,128)S(1)}, u32[]{:S(2)}, u32[]{:S(2)}) collective-permute-start(f32[144,512]{1,0:T(8,128)S(1)} %fusion.1), channel_id=1, source_target_pairs={{0,4},{1,5},{2,6},{3,7},{4,0},{5,1},{6,2},{7,3},{8,12},{9,13},{10,... | collective-permute-start | bytes 884744 | tf_op jit(solution)/shard_map/ppermute | solution.py:13
  177.2 14.2 %collective-permute-done.2 = f32[144,512]{1,0:T(8,128)S(1)} collective-permute-done((f32[144,512]{1,0:T(8,128)S(1)}, f32[144,512]{1,0:T(8,128)S(1)}, u32[]{:S(2)}, u32[]{:S(2)}) %collective-permute-start.2) | collective-permute-done | bytes 294944 | tf_op jit(solution)/shard_map/ppermute | solution.py:13
  191.4 0.8 add.64
  192.1 0.0 all-gather.9.cloned.1.call-update
  192.2 0.0 all-gather.11.cloned.1.call-start
  192.2 38.9 %all-gather.9.cloned.1.call-done = f32[576,512]{1,0:T(8,128)} async-done(((f32[144,512]{1,0:T(8,128)}), f32[576,512]{1,0:T(8,128)}) %all-gather.9.cloned.1.call-update) | async-done | bytes 1179664 | tf_op jit(solution)/shard_map/all_gather | solution.py:87
  231.1 0.0 all-gather.11.cloned.1.call-update
  231.1 22.1 %all-gather.11.cloned.1.call-done = f32[1152,512]{1,0:T(8,128)} async-done(((f32[576,512]{1,0:T(8,128)}), f32[1152,512]{1,0:T(8,128)}) %all-gather.11.cloned.1.call-update) | async-done | bytes 2359312 | tf_op jit(solution)/shard_map/all_gather | solution.py:88
  253.2 3.3 %copy.18 = f32[1,2,576,512]{3,2,1,0:T(8,128)} copy(f32[1,2,576,512]{3,2,1,0:T(8,128)} %bitcast.46) | data formatting | bytes 4718592
  (5 shorter events, 0.1 us)
Async XLA Ops:
  7.2 51.1 %copy-start = (bf16[1,1,128,512]{3,2,1,0:T(8,128)(2,1)S(1)}, bf16[1,1,128,512]{3,2,1,0:T(8,128)(2,1)}, u32[]{:S(2)}) copy-start(bf16[1,1,128,512]{3,2,1,0:T(8,128)(2,1)} %param.14) | copy-start | bytes 393220
  7.2 50.0 %all-gather.5.cloned.1.call-start = ((), (), s32[]{:S(2)}) async-start(), calls=%async_computation.2 | async-start | bytes 1638400 | tf_op jit(solution)/shard_map/all_gather | solution.py:74
  8.8 48.5 %copy-start.5 = (s32[1,1,128]{2,1,0:T(1,128)S(1)}, s32[1,1,128]{2,1,0:T(1,128)}, u32[]{:S(2)}) copy-start(s32[1,1,128]{2,1,0:T(1,128)} %param.13) | copy-start | bytes 1540
  11.5 46.7 %copy-start.3 = (f32[3,1,1,128]{3,2,1,0:T(1,128)S(1)}, f32[3,1,1,128]{3,2,1,0:T(1,128)}, u32[]{:S(2)}) copy-start(f32[3,1,1,128]{3,2,1,0:T(1,128)} %param.9) | copy-start | bytes 4612
  11.6 68.2 %all-gather.7.cloned.1.call-start = ((), (), s32[]{:S(2)}) async-start(), calls=%async_computation.3 | async-start | bytes 3932160 | tf_op jit(solution)/shard_map/all_gather | solution.py:75
  57.2 51.7 %reduce-scatter.3.cloned.1.call-start = ((), (), s32[]{:S(2)}) async-start(), calls=%async_computation.4 | async-start | bytes 3538944 | tf_op jit(solution)/shard_map/reduce_scatter | solution.py:84
  58.2 24.7 %copy-start.2 = (bf16[576,1,1,128]{3,0,2,1:T(8,128)(2,1)S(1)}, bf16[576,1,1,128]{3,0,2,1:T(8,128)(2,1)}, u32[]{:S(2)}) copy-start(bf16[576,1,1,128]{3,0,2,1:T(8,128)(2,1)} %param.12) | copy-start | bytes 442372
  58.2 24.7 %copy-start.4 = (f32[1,1,128]{2,1,0:T(1,128)S(1)}, f32[1,1,128]{2,1,0:T(1,128)}, u32[]{:S(2)}) copy-start(f32[1,1,128]{2,1,0:T(1,128)} %param.10) | copy-start | bytes 1540
  89.6 59.3 %copy-start.1 = (bf16[1,3,512,512]{3,2,1,0:T(8,128)(2,1)S(1)}, bf16[1,3,512,512]{3,2,1,0:T(8,128)(2,1)}, u32[]{:S(2)}) copy-start(bf16[1,3,512,512]{3,2,1,0:T(8,128)(2,1)} %param.15) | copy-start | bytes 4718596
  89.6 59.2 %reduce-scatter.5.cloned.1.call-start = ((), (), s32[]{:S(2)}) async-start(), calls=%async_computation.5 | async-start | bytes 1474560 | tf_op jit(solution)/shard_map/reduce_scatter | solution.py:85
  109.0 122.2 %all-gather.9.cloned.1.call-start = ((), (), s32[]{:S(2)}) async-start(), calls=%async_computation.6 | async-start | bytes 1474560 | tf_op jit(solution)/shard_map/all_gather | solution.py:87
  150.2 9.6 %collective-permute-start = (f32[144,512]{1,0:T(8,128)S(1)}, f32[144,512]{1,0:T(8,128)S(1)}, u32[]{:S(2)}, u32[]{:S(2)}) collective-permute-start(f32[144,512]{1,0:T(8,128)S(1)} %fusion.5), channel_id=1, source_target_pairs={{0,1},{1,0},{2,3},{3,2},{4,5},{5,4},{6,7},{7,6},{8,9},{9,8},{10,11... | collective-permute-start | bytes 884744 | tf_op jit(solution)/shard_map/ppermute | solution.py:13
  160.2 10.2 %collective-permute-start.1 = (f32[144,512]{1,0:T(8,128)S(1)}, f32[144,512]{1,0:T(8,128)S(1)}, u32[]{:S(2)}, u32[]{:S(2)}) collective-permute-start(f32[144,512]{1,0:T(8,128)S(1)} %fusion.3), channel_id=1, source_target_pairs={{0,2},{1,3},{2,0},{3,1},{4,6},{5,7},{6,4},{7,5},{8,10},{9,11},{10,... | collective-permute-start | bytes 884744 | tf_op jit(solution)/shard_map/ppermute | solution.py:13
  170.8 20.5 %collective-permute-start.2 = (f32[144,512]{1,0:T(8,128)S(1)}, f32[144,512]{1,0:T(8,128)S(1)}, u32[]{:S(2)}, u32[]{:S(2)}) collective-permute-start(f32[144,512]{1,0:T(8,128)S(1)} %fusion.1), channel_id=1, source_target_pairs={{0,4},{1,5},{2,6},{3,7},{4,0},{5,1},{6,2},{7,3},{8,12},{9,13},{10,... | collective-permute-start | bytes 884744 | tf_op jit(solution)/shard_map/ppermute | solution.py:13
  192.2 61.1 %all-gather.11.cloned.1.call-start = ((), (), s32[]{:S(2)}) async-start(), calls=%async_computation.7 | async-start | bytes 3538944 | tf_op jit(solution)/shard_map/all_gather | solution.py:88
Sparse Core Ops, SparseCore 0:
  11.7 45.4 all-gather.4
  59.3 20.4 all-gather.6
  89.8 19.1 reduce-scatter.2
  111.9 36.9 reduce-scatter.4
  192.3 38.7 all-gather.8
  233.3 19.9 all-gather.10
where the time goes:
time: 264 us; the launch traced here: 263 us
  waiting for transfers between devices  213 us (81%)
  between operations  14.3 us (5%)
  starting transfers between devices  14.2 us (5%)
  local copies, waits for them, and re-layouts  11 us (4%)
  matrix products  6.58 us (2%)
  other arithmetic  4.07 us (2%)
    all_gather x1, waiting for transfers between devices, shards(): piece = lax.all_gather(outgoing, 'ylo', axis=1, tiled=True)  45.6 us
    reduce_scatter x1, waiting for transfers between devices, shards(): mine = lax.psum_scatter(mine, 'ylo', scatter_dimension=0, tiled=True)  39.9 us
    all_gather x1, waiting for transfers between devices, shards(): top = lax.all_gather(top, 'ylo', axis=0, tiled=True)  38.9 us
    ppermute x3, waiting for transfers between devices, partner(): return lax.ppermute(value, axis, pairs)  26.3 us
    all_gather x1, waiting for transfers between devices, shards(): lax.all_gather(top, 'core', axis=0, tiled=True)  22.1 us
    all_gather x1, waiting for transfers between devices, shards(): piece = lax.all_gather(piece, 'core', axis=1, tiled=True)  21.1 us
    reduce_scatter x1, waiting for transfers between devices, shards(): mine = lax.psum_scatter(stacked, 'core', scatter_dimension=0, tiled=True)  19.3 us
    ppermute x3, starting transfers between devices, partner(): return lax.ppermute(value, axis, pairs)  14 us
  transfers between devices with their start and end apart: 9, of which 9 were waited for; matrix products, arithmetic and copies ran while one was open for 0% of the time, Pallas kernels for 0%

commit v1 on v0

--- a/solution.py
+++ b/solution.py
@@ -72,7 +72,9 @@
     )
     outgoing = jnp.concatenate([coords, area_row, scaled.astype(jnp.float32)], axis=0)
     piece = lax.all_gather(outgoing, "ylo", axis=1, tiled=True)
-    piece = lax.all_gather(piece, "core", axis=1, tiled=True)
+    piece = jnp.concatenate(
+        lax.all_to_all(jnp.stack([piece] * lax.axis_size("core")), "core", 0, 0), axis=1
+    )
     near_sum = near_block(coords, area_row[0], piece[:3], piece[3], piece[4:].astype(jnp.bfloat16))
     offdiag = (full_sketch.reshape(probe_count, panels).astype(jnp.float32) - near_sum).astype(
         jnp.bfloat16

time: 264 us -> 248 us (0.939)
  waiting for transfers between devices: 213 us -> 189 us
  blocking collectives: 0 us -> 7.4 us
    all_gather x1 -> x0, waiting for transfers between devices: 21.1 us -> none  [shards(): piece = lax.all_gather(piece, 'core', axis=1, tiled=True)]
    all_to_all x0 -> x1, blocking collectives: none -> 7.4 us  [shards(): lax.all_to_all(jnp.stack([piece] * lax.axis_size('core')), 'core', 0, 0)]
    slice x1, local copies, waits for them, and re-layouts: 3.15 us -> 0.01 us  [kernel_tile(): gap = target_pos[component][:, None] - source_pos[component][None, :]]
    unnamed x15 -> x18, local copies, waits for them, and re-layouts: 5.16 us -> 6.3 us
  transfers between devices with their start and end apart: 9 -> 8, of which waited for: 9 -> 8; matrix products, arithmetic and copies ran while one was open for 0% -> 1% of each run, Pallas kernels for 0% -> 0%
where the time goes in v1:
time: 248 us; the launch traced here: 247 us
  waiting for transfers between devices  189 us (76%)
  starting transfers between devices  14.3 us (6%)
  between operations  14 us (6%)
  local copies, waits for them, and re-layouts  11.2 us (5%)
  blocking collectives  7.4 us (3%)
  other arithmetic  6.04 us (2%)
  matrix products  5.38 us (2%)
    all_gather x1, waiting for transfers between devices, shards(): piece = lax.all_gather(outgoing, 'ylo', axis=1, tiled=True)  43.2 us
    reduce_scatter x1, waiting for transfers between devices, shards(): mine = lax.psum_scatter(mine, 'ylo', scatter_dimension=0, tiled=True)  40 us
    all_gather x1, waiting for transfers between devices, shards(): top = lax.all_gather(top, 'ylo', axis=0, tiled=True)  39 us
    ppermute x3, waiting for transfers between devices, partner(): return lax.ppermute(value, axis, pairs)  26.1 us
    all_gather x1, waiting for transfers between devices, shards(): lax.all_gather(top, 'core', axis=0, tiled=True)  22.1 us
    reduce_scatter x1, waiting for transfers between devices, shards(): mine = lax.psum_scatter(stacked, 'core', scatter_dimension=0, tiled=True)  18.4 us
    ppermute x3, starting transfers between devices, partner(): return lax.ppermute(value, axis, pairs)  14.1 us
    all_to_all x1, blocking collectives, shards(): lax.all_to_all(jnp.stack([piece] * lax.axis_size('core')), 'core', 0, 0)  7.4 us
  transfers between devices with their start and end apart: 8, of which 8 were waited for; matrix products, arithmetic and copies ran while one was open for 1% of the time, Pallas kernels for 0%

profile of v1, /device:TPU:1, one launch (start us, length us, event | category | flops | bytes accessed | tf_op | source)
XLA Modules:
  0.0 247.1 jit_solution(4932087240912312485)
XLA Ops:
  7.2 0.0 copy-start
  7.2 0.0 copy-start.6
  7.2 0.0 all-gather.4.cloned.1.call-start
  7.2 1.1 copy.23
  8.3 0.0 copy-start.4
  8.3 0.9 copy.22
  9.2 0.8 copy.24
  9.9 0.7 fusion.26
  10.7 0.9 pad_maximum_fusion.2
  11.6 0.0 all-gather.4.cloned.1.call-update
  11.6 0.0 reduce-scatter.3.cloned.1.call-start
  11.7 0.0 copy-done.6
  11.7 0.9 gather_fusion.1
  12.6 0.0 copy-done.4
  12.6 0.0 copy-done
  12.6 1.4 fusion.27
  14.1 43.2 %all-gather.4.cloned.1.call-done = f32[580,512]{0,1:T(8,128)} async-done(((f32[580,128]{0,1:T(8,128)}), f32[580,512]{0,1:T(8,128)}) %all-gather.4.cloned.1.call-update) | async-done | bytes 1187856 | tf_op jit(solution)/shard_map/all_gather | solution.py:74
  57.2 2.0 pad_maximum_fusion
  59.2 2.0 copy.25
  61.2 7.4 %all_to_all.5 = f32[2,580,512]{2,1,0:T(8,128)S(1)} all-to-all(f32[2,580,512]{2,1,0:T(8,128)} %copy.25), channel_id=1, replica_groups=mesh['ylo'=4,'core'=2,'leaf'=64] {'core'}, dimensions={0} | all-to-all | bytes 4751360 | tf_op jit(solution)/shard_map/all_to_all | solution.py:76
  68.7 0.3 fusion
  69.0 0.0 copy-start.3
  69.0 0.0 copy-start.5
  69.0 0.2 copy.28
  69.2 0.7 copy-done.3
  69.9 0.0 copy-done.5
  69.9 1.4 fusion.10
  71.3 0.0 copy-start.1
  71.3 0.2 copy.27
  71.5 0.9 gather_fusion
  72.4 0.4 fusion.29
  72.8 0.0 copy-done.1
  72.8 1.6 pad_maximum_fusion.1
  74.4 0.0 copy-start.2
  74.4 0.0 reduce-scatter.3.cloned.1.call-update
  74.5 0.0 reduce-scatter.5.cloned.1.call-start
  74.5 18.4 %reduce-scatter.3.cloned.1.call-done = f32[576,512]{1,0:T(8,128)} async-done(((f32[1152,512]{1,0:T(8,128)}), f32[576,512]{1,0:T(8,128)}) %reduce-scatter.3.cloned.1.call-update) | async-done | bytes 1179664 | tf_op jit(solution)/shard_map/reduce_scatter | solution.py:86
  92.9 0.0 reduce-scatter.5.cloned.1.call-update
  92.9 0.0 all-gather.6.cloned.1.call-start
  92.9 40.0 %reduce-scatter.5.cloned.1.call-done = f32[144,512]{1,0:T(8,128)} async-done(((f32[576,512]{1,0:T(8,128)}), f32[144,512]{1,0:T(8,128)}) %reduce-scatter.5.cloned.1.call-update) | async-done | bytes 294928 | tf_op jit(solution)/shard_map/reduce_scatter | solution.py:87
  132.9 0.0 copy-done.2
  132.9 1.4 fusion.5
  134.3 3.1 %collective-permute-start = (f32[144,512]{1,0:T(8,128)S(1)}, f32[144,512]{1,0:T(8,128)S(1)}, u32[]{:S(2)}, u32[]{:S(2)}) collective-permute-start(f32[144,512]{1,0:T(8,128)S(1)} %fusion.5), channel_id=1, source_target_pairs={{0,1},{1,0},{2,3},{3,2},{4,5},{5,4},{6,7},{7,6},{8,9},{9,8},{10,11... | collective-permute-start | bytes 884744 | tf_op jit(solution)/shard_map/ppermute | solution.py:13
  137.4 6.5 %collective-permute-done = f32[144,512]{1,0:T(8,128)S(1)} collective-permute-done((f32[144,512]{1,0:T(8,128)S(1)}, f32[144,512]{1,0:T(8,128)S(1)}, u32[]{:S(2)}, u32[]{:S(2)}) %collective-permute-start) | collective-permute-done | bytes 294944 | tf_op jit(solution)/shard_map/ppermute | solution.py:13
  143.9 0.4 fusion.3
  144.3 4.6 %collective-permute-start.1 = (f32[144,512]{1,0:T(8,128)S(1)}, f32[144,512]{1,0:T(8,128)S(1)}, u32[]{:S(2)}, u32[]{:S(2)}) collective-permute-start(f32[144,512]{1,0:T(8,128)S(1)} %fusion.3), channel_id=1, source_target_pairs={{0,2},{1,3},{2,0},{3,1},{4,6},{5,7},{6,4},{7,5},{8,10},{9,11},{10,... | collective-permute-start | bytes 884744 | tf_op jit(solution)/shard_map/ppermute | solution.py:13
  148.9 5.5 %collective-permute-done.1 = f32[144,512]{1,0:T(8,128)S(1)} collective-permute-done((f32[144,512]{1,0:T(8,128)S(1)}, f32[144,512]{1,0:T(8,128)S(1)}, u32[]{:S(2)}, u32[]{:S(2)}) %collective-permute-start.1) | collective-permute-done | bytes 294944 | tf_op jit(solution)/shard_map/ppermute | solution.py:13
  154.4 0.4 fusion.1
  154.8 6.4 %collective-permute-start.2 = (f32[144,512]{1,0:T(8,128)S(1)}, f32[144,512]{1,0:T(8,128)S(1)}, u32[]{:S(2)}, u32[]{:S(2)}) collective-permute-start(f32[144,512]{1,0:T(8,128)S(1)} %fusion.1), channel_id=1, source_target_pairs={{0,4},{1,5},{2,6},{3,7},{4,0},{5,1},{6,2},{7,3},{8,12},{9,13},{10,... | collective-permute-start | bytes 884744 | tf_op jit(solution)/shard_map/ppermute | solution.py:13
  161.2 14.1 %collective-permute-done.2 = f32[144,512]{1,0:T(8,128)S(1)} collective-permute-done((f32[144,512]{1,0:T(8,128)S(1)}, f32[144,512]{1,0:T(8,128)S(1)}, u32[]{:S(2)}, u32[]{:S(2)}) %collective-permute-start.2) | collective-permute-done | bytes 294944 | tf_op jit(solution)/shard_map/ppermute | solution.py:13
  175.3 0.8 add.64
  176.1 0.0 all-gather.6.cloned.1.call-update
  176.1 0.0 all-gather.8.cloned.1.call-start
  176.2 39.0 %all-gather.6.cloned.1.call-done = f32[576,512]{1,0:T(8,128)} async-done(((f32[144,512]{1,0:T(8,128)}), f32[576,512]{1,0:T(8,128)}) %all-gather.6.cloned.1.call-update) | async-done | bytes 1179664 | tf_op jit(solution)/shard_map/all_gather | solution.py:89
  215.2 0.0 all-gather.8.cloned.1.call-update
  215.2 22.1 %all-gather.8.cloned.1.call-done = f32[1152,512]{1,0:T(8,128)} async-done(((f32[576,512]{1,0:T(8,128)}), f32[1152,512]{1,0:T(8,128)}) %all-gather.8.cloned.1.call-update) | async-done | bytes 2359312 | tf_op jit(solution)/shard_map/all_gather | solution.py:90
  237.3 3.3 %copy.30 = f32[1,2,576,512]{3,2,1,0:T(8,128)} copy(f32[1,2,576,512]{3,2,1,0:T(8,128)} %bitcast.58) | data formatting | bytes 4718592
  (6 shorter events, 0.1 us)
Async XLA Ops:
  7.2 5.5 %copy-start = (bf16[1,1,128,512]{3,2,1,0:T(8,128)(2,1)S(1)}, bf16[1,1,128,512]{3,2,1,0:T(8,128)(2,1)}, u32[]{:S(2)}) copy-start(bf16[1,1,128,512]{3,2,1,0:T(8,128)(2,1)} %param.14) | copy-start | bytes 393220
  7.2 4.5 %copy-start.6 = (s32[1,1,128]{2,1,0:T(1,128)S(1)}, s32[1,1,128]{2,1,0:T(1,128)}, u32[]{:S(2)}) copy-start(s32[1,1,128]{2,1,0:T(1,128)} %param.13) | copy-start | bytes 1540
  7.2 50.1 %all-gather.4.cloned.1.call-start = ((), (), s32[]{:S(2)}) async-start(), calls=%async_computation.3 | async-start | bytes 1638400 | tf_op jit(solution)/shard_map/all_gather | solution.py:74
  8.3 4.3 %copy-start.4 = (f32[3,1,1,128]{3,2,1,0:T(1,128)S(1)}, f32[3,1,1,128]{3,2,1,0:T(1,128)}, u32[]{:S(2)}) copy-start(f32[3,1,1,128]{3,2,1,0:T(1,128)} %param.9) | copy-start | bytes 4612
  11.6 81.2 %reduce-scatter.3.cloned.1.call-start = ((), (), s32[]{:S(2)}) async-start(), calls=%async_computation.4 | async-start | bytes 3538944 | tf_op jit(solution)/shard_map/reduce_scatter | solution.py:86
  69.0 0.9 copy-start.3
  69.0 0.9 copy-start.5
  71.3 1.5 copy-start.1
  74.4 58.5 %copy-start.2 = (bf16[1,3,512,512]{3,2,1,0:T(8,128)(2,1)S(1)}, bf16[1,3,512,512]{3,2,1,0:T(8,128)(2,1)}, u32[]{:S(2)}) copy-start(bf16[1,3,512,512]{3,2,1,0:T(8,128)(2,1)} %param.15) | copy-start | bytes 4718596
  74.5 58.5 %reduce-scatter.5.cloned.1.call-start = ((), (), s32[]{:S(2)}) async-start(), calls=%async_computation.5 | async-start | bytes 1474560 | tf_op jit(solution)/shard_map/reduce_scatter | solution.py:87
  92.9 122.3 %all-gather.6.cloned.1.call-start = ((), (), s32[]{:S(2)}) async-start(), calls=%async_computation.6 | async-start | bytes 1474560 | tf_op jit(solution)/shard_map/all_gather | solution.py:89
  134.3 9.6 %collective-permute-start = (f32[144,512]{1,0:T(8,128)S(1)}, f32[144,512]{1,0:T(8,128)S(1)}, u32[]{:S(2)}, u32[]{:S(2)}) collective-permute-start(f32[144,512]{1,0:T(8,128)S(1)} %fusion.5), channel_id=1, source_target_pairs={{0,1},{1,0},{2,3},{3,2},{4,5},{5,4},{6,7},{7,6},{8,9},{9,8},{10,11... | collective-permute-start | bytes 884744 | tf_op jit(solution)/shard_map/ppermute | solution.py:13
  144.3 10.2 %collective-permute-start.1 = (f32[144,512]{1,0:T(8,128)S(1)}, f32[144,512]{1,0:T(8,128)S(1)}, u32[]{:S(2)}, u32[]{:S(2)}) collective-permute-start(f32[144,512]{1,0:T(8,128)S(1)} %fusion.3), channel_id=1, source_target_pairs={{0,2},{1,3},{2,0},{3,1},{4,6},{5,7},{6,4},{7,5},{8,10},{9,11},{10,... | collective-permute-start | bytes 884744 | tf_op jit(solution)/shard_map/ppermute | solution.py:13
  154.8 20.5 %collective-permute-start.2 = (f32[144,512]{1,0:T(8,128)S(1)}, f32[144,512]{1,0:T(8,128)S(1)}, u32[]{:S(2)}, u32[]{:S(2)}) collective-permute-start(f32[144,512]{1,0:T(8,128)S(1)} %fusion.1), channel_id=1, source_target_pairs={{0,4},{1,5},{2,6},{3,7},{4,0},{5,1},{6,2},{7,3},{8,12},{9,13},{10,... | collective-permute-start | bytes 884744 | tf_op jit(solution)/shard_map/ppermute | solution.py:13
  176.1 61.2 %all-gather.8.cloned.1.call-start = ((), (), s32[]{:S(2)}) async-start(), calls=%async_computation.7 | async-start | bytes 3538944 | tf_op jit(solution)/shard_map/all_gather | solution.py:90
Sparse Core Ops, SparseCore 0:
  11.7 45.4 all-gather.3
  74.6 18.2 reduce-scatter.2
  96.0 36.8 reduce-scatter.4
  176.2 38.8 all-gather.5
  217.3 19.9 all-gather.7
